TPU v7x, 32 devices: a whole 2x2x4 slice. The times are simulated.
32 devices in a mesh: row: 8 (over z, y), col: 4 (over x, core).
Axes of the slice: x: 2, y: 2, z: 4, core: 2. Of those that a mesh axis runs over, the one named last changes fastest.
Arguments:
- activations: bfloat16 [512, 28672], P('col', 'row'), may hold values from -36 to 36
- output_gradient: bfloat16 [512, 8192], P('row', 'col'), may hold values from -6 to 6
- frozen_weight: bfloat16 [28672, 8192], P('row', 'col'), may hold values from -0.0390625 to 0.0390625
- sparsity_mask_pattern: int32 [7168, 8192], P('row', 'col'), may hold values from 0 to 5
- adapter_left_factor: bfloat16 [28672, 16], P('row'), may hold values from -0.19921875 to 0.19921875
- adapter_right_factor: bfloat16 [16, 8192], P(None, 'col'), may hold values from -0.359375 to 0.359375
Outputs:
- input_grad: bfloat16 [512, 28672], P('col', 'row')
- left_grad: float32 [28672, 16], P('row')
- right_grad: float32 [16, 8192], P(None, 'col')
Inputs may be any that keep to these rules, and one draw needn't show every extreme that they name: `sparsity_mask_pattern`: a pattern number of the 2:4 mask.
All inputs are finite; a program needn't handle non-finite values.
Results may differ from a plain program's by a relative error of at most 0.005.
Values may be sent and summed in bfloat16 or wider, within the bound.
No kernel may reach another device: no remote copies, remote signals or barrier semaphores. Data moves between devices by JAX's collectives and lax.ppermute only.
A program may use at most 192 MiB of HBM per device.

v0:
```python
import jax
import jax.numpy as jnp
from jax import lax
from jax.sharding import PartitionSpec as P

PAIRS = ((0, 1), (0, 2), (0, 3), (1, 2), (1, 3), (2, 3))
ADAPTER_SCALE = 2.0


def expand_mask(code):
    groups = []
    for column in range(4):
        kept = jnp.zeros(code.shape, jnp.float32)
        for pattern in range(6):
            if column in PAIRS[pattern]:
                kept = kept + (code == pattern).astype(jnp.float32)
        groups.append(kept)
    stacked = jnp.stack(groups, axis=1)
    return stacked.reshape(code.shape[0] * 4, code.shape[1])


def input_sums_of(grad_rows, merged):
    return lax.psum_scatter(
        lax.dot_general(
            grad_rows, merged, (((1,), (1,)), ((), ())), preferred_element_type=jnp.float32
        ),
        "col",
        scatter_dimension=0,
        tiled=True,
    )


def weight_grad_of(activations, grad_rows):
    return lax.dot_general(
        lax.all_gather(activations, "col", axis=0, tiled=True),
        grad_rows,
        (((0,), (0,)), ((), ())),
        preferred_element_type=jnp.float32,
    )


def per_device(
    activations,
    output_gradient,
    frozen_weight,
    sparsity_mask_pattern,
    adapter_left_factor,
    adapter_right_factor,
):
    masked = expand_mask(sparsity_mask_pattern)
    low_rank_update = jnp.dot(
        adapter_left_factor, adapter_right_factor, preferred_element_type=jnp.float32
    )
    merged = (
        masked * (frozen_weight.astype(jnp.float32) + ADAPTER_SCALE * low_rank_update)
    ).astype(jnp.bfloat16)
    grad_rows = lax.all_gather(output_gradient, "row", axis=0, tiled=True)
    all_tokens = grad_rows.shape[0]
    first_grad = weight_grad_of(activations, grad_rows)
    weight_grad, later_grads = lax.optimization_barrier((first_grad, grad_rows))
    input_grad = input_sums_of(later_grads, merged).astype(jnp.bfloat16)
    pruned_gradient = (masked * weight_grad / all_tokens).astype(jnp.bfloat16)
    left_partial = ADAPTER_SCALE * lax.dot_general(
        pruned_gradient,
        adapter_right_factor,
        (((1,), (1,)), ((), ())),
        preferred_element_type=jnp.float32,
    )
    right_partial = ADAPTER_SCALE * lax.dot_general(
        adapter_left_factor,
        pruned_gradient,
        (((0,), (0,)), ((), ())),
        preferred_element_type=jnp.float32,
    )
    right_grad = lax.psum(right_partial, "row")
    left_grad = lax.psum(left_partial, "col")
    return (input_grad, left_grad, right_grad)


def solution(mesh):
    in_specs = (
        P("col", "row"),
        P("row", "col"),
        P("row", "col"),
        P("row", "col"),
        P("row", None),
        P(None, "col"),
    )
    out_specs = (P("col", "row"), P("row", None), P(None, "col"))
    return jax.shard_map(
        per_device, mesh=mesh, in_specs=in_specs, out_specs=out_specs, check_vma=False
    )
```

profile of v0, /device:TPU:0, one launch (start us, length us, event | category | flops | bytes accessed | tf_op | source)
XLA Modules:
  0.0 334.8 jit_solution(17214782488458227821)
XLA Ops:
  7.2 0.0 copy-start
  7.2 0.0 all-gather.5.cloned.1.call-start
  7.2 0.7 all-gather.5.cloned.1.call-update
  7.9 0.0 all-gather.3.cloned.1.call-start
  8.0 0.7 all-gather.3.cloned.1.call-update
  8.7 0.0 reduce-scatter.2.cloned.1.call-start
  8.7 0.0 slice-start
  8.7 7.8 %fusion = (f32[896,1,2048]{2,0,1:T(8,128)S(1)}, pred[896,2048]{1,0:T(8,128)(4,1)S(1)}, pred[896,2048]{1,0:T(8,128)(4,1)S(1)}, pred[896,2048]{1,0:T(8,128)(4,1)}) fusion(s32[896,2048]{1,0:T(8,128)} %param.9), kind=kLoop, calls=%fused_computation.11 | loop fusion | flops 14680064 | bytes 20185088 | tf_op jit(solution)/shard_map/stack | solution.py:18
  16.5 0.0 slice-start.1
  16.6 6.5 %fusion.1 = (f32[896,1,2048]{2,0,1:T(8,128)S(1)}, pred[896,2048]{1,0:T(8,128)(4,1)S(1)}, pred[896,2048]{1,0:T(8,128)(4,1)}) fusion(pred[896,2048]{1,0:T(8,128)(4,1)S(1)} %get-tuple-element.8, s32[896,2048]{1,0:T(8,128)} %param.9), kind=kLoop, calls=%fused_computation.12 | loop fusion | flops 12845056 | bytes 20185088 | tf_op jit(solution)/shard_map/stack | solution.py:18
  23.1 0.0 slice-done
  23.1 0.0 slice-done.1
  23.1 3.6 %fusion.2 = (f32[896,1,2048]{2,0,1:T(8,128)S(1)}, pred[896,2048]{1,0:T(8,128)(4,1)}) fusion(pred[896,2048]{1,0:T(8,128)(4,1)S(1)} %get-tuple-element.12, pred[896,2048]{1,0:T(8,128)(4,1)S(1)} %get-tuple-element.9, s32[896,2048]{1,0:T(8,128)S(1)} %bitcast.20), kind=kLoop, calls=%fused_computation.13 | loop fusion | flops 11010048 | bytes 20185088 | tf_op jit(solution)/shard_map/stack | solution.py:18
  26.7 5.1 %fusion.3 = f32[896,1,2048]{2,0,1:T(8,128)S(1)} fusion(pred[896,2048]{1,0:T(8,128)(4,1)} %get-tuple-element.15, pred[896,2048]{1,0:T(8,128)(4,1)} %get-tuple-element.13, pred[896,2048]{1,0:T(8,128)(4,1)} %get-tuple-element.10), kind=kLoop, calls=%fused_computation.14 | loop fusion | flops 9175040 | bytes 12845056 | tf_op jit(solution)/shard_map/stack | solution.py:18
  31.8 10.3 %pad_maximum_fusion = f32[896,4,2048]{2,0,1:T(8,128)} fusion(f32[896,1,2048]{2,0,1:T(8,128)S(1)} %fusion.3, f32[896,1,2048]{2,0,1:T(8,128)S(1)} %get-tuple-element.14, f32[896,1,2048]{2,0,1:T(8,128)S(1)} %get-tuple-element.11, f32[896,1,2048]{2,0,1:T(8,128)S(1)} %get-tuple-element.7), kind=kLoop, calls=%fused_computation | loop fusion | flops 22020096 | bytes 58720256 | tf_op jit(solution)/shard_map/stack | solution.py:18
  42.1 33.6 %copy.9 = f32[896,4,2048]{2,1,0:T(4,128)} copy(f32[896,4,2048]{2,0,1:T(8,128)} %pad_maximum_fusion) | data formatting | bytes 58720256 | tf_op jit(solution)/shard_map/stack | solution.py:18
  75.7 33.5 %reshape.9 = f32[3584,2048]{1,0:T(8,128)} reshape(f32[896,4,2048]{2,1,0:T(4,128)} %copy.9) | data formatting | bytes 58720256 | tf_op jit(solution)/shard_map/reshape | solution.py:19
  109.2 0.0 copy-start.1
  109.2 0.0 all-gather.5.cloned.1.call-done
  109.2 0.0 copy-start.2
  109.2 0.0 all-gather.3.cloned.1.call-done
  109.2 16.2 %fusion.7 = f32[3584,2048]{1,0:T(8,128)} fusion(bf16[512,3584]{1,0:T(8,128)(2,1)} %all-gather.3.cloned.1.call-done, bf16[512,2048]{1,0:T(8,128)(2,1)} %all-gather.5.cloned.1.call-done), kind=kOutput, calls=%fused_computation.26 | convolution fusion | flops 7516192768 | bytes 35127296 | tf_op jit(solution)/shard_map/dot_general | solution.py:34
  125.4 0.0 copy-done
  125.4 0.0 copy-done.1
  125.4 0.0 copy-done.2
  125.4 21.5 %fusion.4 = f32[512,3584]{1,0:T(8,128)} fusion(bf16[512,2048]{1,0:T(8,128)(2,1)S(1)} %copy-done.2, f32[3584,2048]{1,0:T(8,128)} %reshape.9, bf16[3584,2048]{1,0:T(8,128)(2,1)} %param.8, bf16[3584,16]{0,1:T(8,128)(2,1)S(1)} %copy-done, bf16[16,2048]{1,0:T(8,128)(2,1)S(1)} %copy-done.1), kind=kOutput, calls=%fused_computation.22 | convolution fusion | flops 7787773952 | bytes 53657600 | tf_op jit(solution)/shard_map/dot_general | solution.py:24
  146.9 0.0 reduce-scatter.2.cloned.1.call-update
  147.0 0.0 all-reduce.3.cloned.1.call-start
  147.0 26.9 %multiply_convert_fusion = bf16[3584,2048]{1,0:T(8,128)(2,1)} fusion(f32[3584,2048]{1,0:T(8,128)} %reshape.9, f32[3584,2048]{1,0:T(8,128)} %fusion.7), kind=kLoop, calls=%fused_computation.1 | loop fusion | flops 22020096 | bytes 73400320 | tf_op jit(solution)/shard_map/convert_element_type | solution.py:62
  173.9 9.9 %convolution_multiply_fusion = f32[3584,16]{0,1:T(8,128)} fusion(bf16[3584,2048]{1,0:T(8,128)(2,1)} %multiply_convert_fusion, bf16[16,2048]{1,0:T(8,128)(2,1)S(1)} %copy-done.1), kind=kOutput, calls=%fused_computation.15 | convolution fusion | flops 234938368 | bytes 14974976 | tf_op jit(solution)/shard_map/dot_general | solution.py:63
  183.8 0.0 all-reduce.3.cloned.1.call-update
  183.8 0.0 all-reduce.5.cloned.1.call-start
  183.9 8.0 %fusion.5 = f32[16,2048]{1,0:T(8,128)} fusion(bf16[3584,16]{0,1:T(8,128)(2,1)S(1)} %copy-done, bf16[3584,2048]{1,0:T(8,128)(2,1)} %multiply_convert_fusion), kind=kOutput, calls=%fused_computation.24 | convolution fusion | flops 234913792 | bytes 14925824 | tf_op jit(solution)/shard_map/dot_general | solution.py:69
  191.9 0.0 all-reduce.5.cloned.1.call-update
  191.9 24.0 %reduce-scatter.2.cloned.1.call-done = f32[128,3584]{1,0:T(8,128)} async-done(((f32[512,3584]{1,0:T(8,128)}), f32[128,3584]{1,0:T(8,128)}) %reduce-scatter.2.cloned.1.call-update) | async-done | bytes 1835024 | tf_op jit(solution)/shard_map/reduce_scatter | solution.py:23
  215.9 2.5 convert_element_type.44
  218.4 32.5 %all-reduce.3.cloned.1.call-done = f32[3584,16]{0,1:T(8,128)} async-done(((f32[3584,16]{0,1:T(8,128)}), f32[3584,16]{0,1:T(8,128)}) %all-reduce.3.cloned.1.call-update) | async-done | bytes 229392 | tf_op jit(solution)/shard_map/psum | solution.py:76
  250.9 74.2 %all-reduce.5.cloned.1.call-done = f32[16,2048]{1,0:T(8,128)} async-done(((f32[16,2048]{1,0:T(8,128)}), f32[16,2048]{1,0:T(8,128)}) %all-reduce.5.cloned.1.call-update) | async-done | bytes 131088 | tf_op jit(solution)/shard_map/psum | solution.py:75
  325.0 1.6 copy.12
  326.7 1.6 copy.13
  (1 shorter events, 0.0 us)
Async XLA Ops:
  7.2 118.2 %copy-start = (bf16[3584,16]{0,1:T(8,128)(2,1)S(1)}, bf16[3584,16]{0,1:T(8,128)(2,1)}, u32[]{:S(2)}) copy-start(bf16[3584,16]{0,1:T(8,128)(2,1)} %param.10) | copy-start | bytes 344068
  7.2 102.0 %all-gather.5.cloned.1.call-start = ((), (), s32[]{:S(2)}) async-start(), calls=%async_computation.2 | async-start | bytes 2359296 | tf_op jit(solution)/shard_map/all_gather | solution.py:57
  7.9 101.3 %all-gather.3.cloned.1.call-start = ((), (), s32[]{:S(2)}) async-start(), calls=%async_computation.1 | async-start | bytes 4587520 | tf_op jit(solution)/shard_map/all_gather | solution.py:35
  8.7 207.2 %reduce-scatter.2.cloned.1.call-start = ((), (), s32[]{:S(2)}) async-start(), calls=%async_computation.3 | async-start | bytes 9175040 | tf_op jit(solution)/shard_map/reduce_scatter | solution.py:23
  8.7 14.4 %slice-start = ((s8[7340032]{0:T(1024)(128)(4,1)}), s8[4194304]{0:T(1024)(128)(4,1)S(1)}, s32[]{:S(2)}) async-start(s8[7340032]{0:T(1024)(128)(4,1)} %bitcast.19), calls=%async_computation.6 | async-start | bytes 8388608
  16.5 6.5 %slice-start.1 = ((s8[7340032]{0:T(1024)(128)(4,1)}), s8[3145728]{0:T(1024)(128)(4,1)S(1)}, s32[]{:S(2)}) async-start(s8[7340032]{0:T(1024)(128)(4,1)} %bitcast.19), calls=%async_computation.7 | async-start | bytes 6291456
  109.2 16.2 %copy-start.1 = (bf16[16,2048]{1,0:T(8,128)(2,1)S(1)}, bf16[16,2048]{1,0:T(8,128)(2,1)}, u32[]{:S(2)}) copy-start(bf16[16,2048]{1,0:T(8,128)(2,1)} %param.11) | copy-start | bytes 196612
  109.2 16.2 %copy-start.2 = (bf16[512,2048]{1,0:T(8,128)(2,1)S(1)}, bf16[512,2048]{1,0:T(8,128)(2,1)}, u32[]{:S(2)}) copy-start(bf16[512,2048]{1,0:T(8,128)(2,1)} %all-gather.5.cloned.1.call-done) | copy-start | bytes 6291460
  147.0 103.9 %all-reduce.3.cloned.1.call-start = ((), (), s32[]{:S(2)}) async-start(), calls=%async_computation.4 | async-start | bytes 458752 | tf_op jit(solution)/shard_map/psum | solution.py:76
  183.8 141.2 %all-reduce.5.cloned.1.call-start = ((), (), s32[]{:S(2)}) async-start(), calls=%async_computation.5 | async-start | bytes 262144 | tf_op jit(solution)/shard_map/psum | solution.py:75
Sparse Core Ops, SparseCore 0:
  10.1 51.8 all-gather.4
  63.5 29.9 all-gather.2
  147.1 68.7 reduce-scatter.1
  218.6 32.1 all-reduce.2
  254.6 70.3 all-reduce.4
where the time goes:
time: 336 us; the launch traced here: 335 us
  waiting for transfers between devices  132 us (39%)
  local copies, waits for them, and re-layouts  70.4 us (21%)
  other arithmetic  62.8 us (19%)
  matrix products  55.6 us (17%)
  between operations  13.8 us (4%)
    psum x1, waiting for transfers between devices, per_device(): right_grad = lax.psum(right_partial, 'row')  74.2 us
    another operation x1, local copies, waits for them, and re-layouts, expand_mask(): stacked = jnp.stack(groups, axis=1)  33.6 us
    reshape x1, local copies, waits for them, and re-layouts, expand_mask(): return stacked.reshape(code.shape[0] * 4, code.shape[1])  33.5 us
    another operation x5, other arithmetic, expand_mask(): stacked = jnp.stack(groups, axis=1)  33.3 us
    psum x1, waiting for transfers between devices, per_device(): left_grad = lax.psum(left_partial, 'col')  32.5 us
    convert_element_type x1, other arithmetic, per_device(): pruned_gradient = (masked * weight_grad / all_tokens).astype(jnp.bfloat16)  26.9 us
    reduce_scatter x1, waiting for transfers between devices, input_sums_of(): lax.psum_scatter(lax.dot_general(grad_rows, merged, (((1,), (1,)), ((), (...  24 us
    dot_general x1, matrix products, input_sums_of(): lax.dot_general(grad_rows, merged, (((1,), (1,)), ((), ())), preferred_el...  21.5 us
  transfers between devices with their start and end apart: 5, of which 3 were waited for; matrix products, arithmetic and copies ran while one was open for 44% of the time, Pallas kernels for 0%

commit v1 on v0

--- a/solution.py
+++ b/solution.py
@@ -73,7 +73,15 @@
         preferred_element_type=jnp.float32,
     )
     right_grad = lax.psum(right_partial, "row")
-    left_grad = lax.psum(left_partial, "col")
+    num = jax.lax.axis_size("col")
+    left_grad, piece_next = (left_partial, 0)
+    while 1 << piece_next < num:
+        nodes = []
+        for to_i in tuple(range(num)):
+            nodes.append((to_i, to_i ^ 1 << piece_next))
+        mid_arr = jax.lax.ppermute(left_grad, "col", perm=nodes)
+        left_grad = left_grad + mid_arr
+        piece_next = piece_next + 1
     return (input_grad, left_grad, right_grad)
 
 

time: 336 us -> 304 us (0.905)
  waiting for transfers between devices: 132 us -> 103 us
  matrix products: 55.6 us -> 49.6 us
  starting transfers between devices: 0.2 us -> 4.14 us
    psum x1 -> x0, waiting for transfers between devices: 32.5 us -> none  [per_device(): left_grad = lax.psum(left_partial, 'col')]
    ppermute x0 -> x2, waiting for transfers between devices: none -> 9.65 us  [per_device(): mid_arr = jax.lax.ppermute(left_grad, 'col', perm=nodes)]
    dot_general x1, matrix products: 8 us -> 2.66 us  [per_device(): lax.dot_general(adapter_left_factor, pruned_gradient, (((0,), (0,)), ((),...]
    ppermute x0 -> x2, starting transfers between devices: none -> 3.98 us  [per_device(): mid_arr = jax.lax.ppermute(left_grad, 'col', perm=nodes)]
    reduce_scatter x1, waiting for transfers between devices: 24 us -> 20.1 us  [input_sums_of(): lax.psum_scatter(lax.dot_general(grad_rows, merged, (((1,), (1,)), ((), (...]
  transfers between devices with their start and end apart: 5 -> 6, of which waited for: 3 -> 4; matrix products, arithmetic and copies ran while one was open for 44% -> 47% of each run, Pallas kernels for 0% -> 0%
where the time goes in v1:
time: 304 us; the launch traced here: 303 us
  waiting for transfers between devices  103 us (34%)
  local copies, waits for them, and re-layouts  68.7 us (23%)
  other arithmetic  63.9 us (21%)
  matrix products  49.6 us (16%)
  between operations  13.8 us (5%)
  starting transfers between devices  4.14 us (1%)
    psum x1, waiting for transfers between devices, per_device(): right_grad = lax.psum(right_partial, 'row')  71.7 us
    another operation x1, local copies, waits for them, and re-layouts, expand_mask(): stacked = jnp.stack(groups, axis=1)  33.6 us
    reshape x1, local copies, waits for them, and re-layouts, expand_mask(): return stacked.reshape(code.shape[0] * 4, code.shape[1])  33.5 us
    another operation x5, other arithmetic, expand_mask(): stacked = jnp.stack(groups, axis=1)  33.3 us
    convert_element_type x1, other arithmetic, per_device(): pruned_gradient = (masked * weight_grad / all_tokens).astype(jnp.bfloat16)  27.3 us
    dot_general x1, matrix products, input_sums_of(): lax.dot_general(grad_rows, merged, (((1,), (1,)), ((), ())), preferred_el...  21.5 us
    reduce_scatter x1, waiting for transfers between devices, input_sums_of(): lax.psum_scatter(lax.dot_general(grad_rows, merged, (((1,), (1,)), ((), (...  20.1 us
    dot_general x1, matrix products, weight_grad_of(): lax.dot_general(lax.all_gather(activations, 'col', axis=0, tiled=True), g...  16.2 us
  transfers between devices with their start and end apart: 6, of which 4 were waited for; matrix products, arithmetic and copies ran while one was open for 47% of the time, Pallas kernels for 0%

profile of v1, /device:TPU:0, one launch (start us, length us, event | category | flops | bytes accessed | tf_op | source)
XLA Modules:
  0.0 303.1 jit_solution(3380820587304936236)
XLA Ops:
  7.2 0.0 copy-start
  7.2 0.0 all-gather.5.cloned.1.call-start
  7.2 0.7 all-gather.5.cloned.1.call-update
  7.9 0.0 all-gather.3.cloned.1.call-start
  8.0 0.7 all-gather.3.cloned.1.call-update
  8.7 0.0 reduce-scatter.2.cloned.1.call-start
  8.7 0.0 slice-start
  8.7 7.8 %fusion = (f32[896,1,2048]{2,0,1:T(8,128)S(1)}, pred[896,2048]{1,0:T(8,128)(4,1)S(1)}, pred[896,2048]{1,0:T(8,128)(4,1)S(1)}, pred[896,2048]{1,0:T(8,128)(4,1)}) fusion(s32[896,2048]{1,0:T(8,128)} %param.9), kind=kLoop, calls=%fused_computation.11 | loop fusion | flops 14680064 | bytes 20185088 | tf_op jit(solution)/shard_map/stack | solution.py:18
  16.5 0.0 slice-start.1
  16.5 6.5 %fusion.1 = (f32[896,1,2048]{2,0,1:T(8,128)S(1)}, pred[896,2048]{1,0:T(8,128)(4,1)S(1)}, pred[896,2048]{1,0:T(8,128)(4,1)}) fusion(pred[896,2048]{1,0:T(8,128)(4,1)S(1)} %get-tuple-element.8, s32[896,2048]{1,0:T(8,128)} %param.9), kind=kLoop, calls=%fused_computation.12 | loop fusion | flops 12845056 | bytes 20185088 | tf_op jit(solution)/shard_map/stack | solution.py:18
  23.0 0.0 slice-done
  23.0 0.0 slice-done.1
  23.0 3.6 %fusion.2 = (f32[896,1,2048]{2,0,1:T(8,128)S(1)}, pred[896,2048]{1,0:T(8,128)(4,1)}) fusion(pred[896,2048]{1,0:T(8,128)(4,1)S(1)} %get-tuple-element.12, pred[896,2048]{1,0:T(8,128)(4,1)S(1)} %get-tuple-element.9, s32[896,2048]{1,0:T(8,128)S(1)} %bitcast.20), kind=kLoop, calls=%fused_computation.13 | loop fusion | flops 11010048 | bytes 20185088 | tf_op jit(solution)/shard_map/stack | solution.py:18
  26.7 5.1 %fusion.3 = f32[896,1,2048]{2,0,1:T(8,128)S(1)} fusion(pred[896,2048]{1,0:T(8,128)(4,1)} %get-tuple-element.15, pred[896,2048]{1,0:T(8,128)(4,1)} %get-tuple-element.13, pred[896,2048]{1,0:T(8,128)(4,1)} %get-tuple-element.10), kind=kLoop, calls=%fused_computation.14 | loop fusion | flops 9175040 | bytes 12845056 | tf_op jit(solution)/shard_map/stack | solution.py:18
  31.8 10.3 %pad_maximum_fusion = f32[896,4,2048]{2,0,1:T(8,128)} fusion(f32[896,1,2048]{2,0,1:T(8,128)S(1)} %fusion.3, f32[896,1,2048]{2,0,1:T(8,128)S(1)} %get-tuple-element.14, f32[896,1,2048]{2,0,1:T(8,128)S(1)} %get-tuple-element.11, f32[896,1,2048]{2,0,1:T(8,128)S(1)} %get-tuple-element.7), kind=kLoop, calls=%fused_computation | loop fusion | flops 22020096 | bytes 58720256 | tf_op jit(solution)/shard_map/stack | solution.py:18
  42.0 33.6 %copy.9 = f32[896,4,2048]{2,1,0:T(4,128)} copy(f32[896,4,2048]{2,0,1:T(8,128)} %pad_maximum_fusion) | data formatting | bytes 58720256 | tf_op jit(solution)/shard_map/stack | solution.py:18
  75.6 33.5 %reshape.9 = f32[3584,2048]{1,0:T(8,128)} reshape(f32[896,4,2048]{2,1,0:T(4,128)} %copy.9) | data formatting | bytes 58720256 | tf_op jit(solution)/shard_map/reshape | solution.py:19
  109.2 0.0 copy-start.2
  109.2 0.0 all-gather.5.cloned.1.call-done
  109.2 0.0 copy-start.3
  109.2 0.0 all-gather.3.cloned.1.call-done
  109.2 16.2 %fusion.7 = f32[3584,2048]{1,0:T(8,128)} fusion(bf16[512,3584]{1,0:T(8,128)(2,1)} %all-gather.3.cloned.1.call-done, bf16[512,2048]{1,0:T(8,128)(2,1)} %all-gather.5.cloned.1.call-done), kind=kOutput, calls=%fused_computation.26 | convolution fusion | flops 7516192768 | bytes 35127296 | tf_op jit(solution)/shard_map/dot_general | solution.py:34
  125.4 0.0 copy-done
  125.4 0.0 copy-done.2
  125.4 0.0 copy-done.3
  125.4 21.5 %fusion.4 = f32[512,3584]{1,0:T(8,128)} fusion(bf16[512,2048]{1,0:T(8,128)(2,1)S(1)} %copy-done.3, f32[3584,2048]{1,0:T(8,128)} %reshape.9, bf16[3584,2048]{1,0:T(8,128)(2,1)} %param.8, bf16[3584,16]{0,1:T(8,128)(2,1)S(1)} %copy-done, bf16[16,2048]{1,0:T(8,128)(2,1)S(1)} %copy-done.2), kind=kOutput, calls=%fused_computation.22 | convolution fusion | flops 7787773952 | bytes 53657600 | tf_op jit(solution)/shard_map/dot_general | solution.py:24
  147.0 0.0 reduce-scatter.2.cloned.1.call-update
  147.0 0.0 all-reduce.2.cloned.1.call-start
  147.0 27.3 %multiply_convert_fusion = bf16[3584,2048]{1,0:T(8,128)(2,1)} fusion(f32[3584,2048]{1,0:T(8,128)} %reshape.9, f32[3584,2048]{1,0:T(8,128)} %fusion.7), kind=kLoop, calls=%fused_computation.1 | loop fusion | flops 22020096 | bytes 73400320 | tf_op jit(solution)/shard_map/convert_element_type | solution.py:62
  174.4 0.0 copy-start.1
  174.4 9.2 %convolution_multiply_fusion = f32[3584,16]{0,1:T(8,128)S(1)} fusion(bf16[3584,2048]{1,0:T(8,128)(2,1)} %multiply_convert_fusion, bf16[16,2048]{1,0:T(8,128)(2,1)S(1)} %copy-done.2), kind=kOutput, calls=%fused_computation.15 | convolution fusion | flops 234938368 | bytes 14974976 | tf_op jit(solution)/shard_map/dot_general | solution.py:63
  183.6 0.4 collective-permute-start
  184.0 1.1 collective-permute-done
  185.1 3.6 %collective-permute-start.1 = (f32[3584,16]{0,1:T(8,128)S(1)}, f32[3584,16]{0,1:T(8,128)S(1)}, u32[]{:S(2)}, u32[]{:S(2)}) collective-permute-start(f32[3584,16]{0,1:T(8,128)S(1)} %add.46), channel_id=1, source_target_pairs={{0,2},{1,3},{2,0},{3,1},{4,6},{5,7},{6,4},{7,5},{8,10},{9,11},{10,... | collective-permute-start | bytes 688136 | tf_op jit(solution)/shard_map/ppermute | solution.py:82
  188.7 0.0 copy-done.1
  188.7 2.7 fusion.5
  191.4 0.0 all-reduce.2.cloned.1.call-update
  191.4 8.5 %collective-permute-done.1 = f32[3584,16]{0,1:T(8,128)S(1)} collective-permute-done((f32[3584,16]{0,1:T(8,128)S(1)}, f32[3584,16]{0,1:T(8,128)S(1)}, u32[]{:S(2)}, u32[]{:S(2)}) %collective-permute-start.1) | collective-permute-done | bytes 229408 | tf_op jit(solution)/shard_map/ppermute | solution.py:82
  199.9 0.7 add.47
  200.6 20.1 %reduce-scatter.2.cloned.1.call-done = f32[128,3584]{1,0:T(8,128)} async-done(((f32[512,3584]{1,0:T(8,128)}), f32[128,3584]{1,0:T(8,128)}) %reduce-scatter.2.cloned.1.call-update) | async-done | bytes 1835024 | tf_op jit(solution)/shard_map/reduce_scatter | solution.py:23
  220.7 2.5 convert_element_type.44
  223.3 71.7 %all-reduce.2.cloned.1.call-done = f32[16,2048]{1,0:T(8,128)} async-done(((f32[16,2048]{1,0:T(8,128)}), f32[16,2048]{1,0:T(8,128)}) %all-reduce.2.cloned.1.call-update) | async-done | bytes 131088 | tf_op jit(solution)/shard_map/psum | solution.py:75
  295.0 1.6 copy.11
  (2 shorter events, 0.0 us)
Async XLA Ops:
  7.2 118.2 %copy-start = (bf16[3584,16]{0,1:T(8,128)(2,1)S(1)}, bf16[3584,16]{0,1:T(8,128)(2,1)}, u32[]{:S(2)}) copy-start(bf16[3584,16]{0,1:T(8,128)(2,1)} %param.10) | copy-start | bytes 344068
  7.2 102.0 %all-gather.5.cloned.1.call-start = ((), (), s32[]{:S(2)}) async-start(), calls=%async_computation.2 | async-start | bytes 2359296 | tf_op jit(solution)/shard_map/all_gather | solution.py:57
  7.9 101.3 %all-gather.3.cloned.1.call-start = ((), (), s32[]{:S(2)}) async-start(), calls=%async_computation.1 | async-start | bytes 4587520 | tf_op jit(solution)/shard_map/all_gather | solution.py:35
  8.7 212.1 %reduce-scatter.2.cloned.1.call-start = ((), (), s32[]{:S(2)}) async-start(), calls=%async_computation.3 | async-start | bytes 9175040 | tf_op jit(solution)/shard_map/reduce_scatter | solution.py:23
  8.7 14.3 %slice-start = ((s8[7340032]{0:T(1024)(128)(4,1)}), s8[4194304]{0:T(1024)(128)(4,1)S(1)}, s32[]{:S(2)}) async-start(s8[7340032]{0:T(1024)(128)(4,1)} %bitcast.19), calls=%async_computation.5 | async-start | bytes 8388608
  16.5 6.5 %slice-start.1 = ((s8[7340032]{0:T(1024)(128)(4,1)}), s8[3145728]{0:T(1024)(128)(4,1)S(1)}, s32[]{:S(2)}) async-start(s8[7340032]{0:T(1024)(128)(4,1)} %bitcast.19), calls=%async_computation.6 | async-start | bytes 6291456
  109.2 16.2 %copy-start.2 = (bf16[16,2048]{1,0:T(8,128)(2,1)S(1)}, bf16[16,2048]{1,0:T(8,128)(2,1)}, u32[]{:S(2)}) copy-start(bf16[16,2048]{1,0:T(8,128)(2,1)} %param.11) | copy-start | bytes 196612
  109.2 16.2 %copy-start.3 = (bf16[512,2048]{1,0:T(8,128)(2,1)S(1)}, bf16[512,2048]{1,0:T(8,128)(2,1)}, u32[]{:S(2)}) copy-start(bf16[512,2048]{1,0:T(8,128)(2,1)} %all-gather.5.cloned.1.call-done) | copy-start | bytes 6291460
  147.0 148.0 %all-reduce.2.cloned.1.call-start = ((), (), s32[]{:S(2)}) async-start(), calls=%async_computation.4 | async-start | bytes 262144 | tf_op jit(solution)/shard_map/psum | solution.py:75
  174.4 14.3 %copy-start.1 = (bf16[3584,2048]{1,0:T(8,128)(2,1)S(1)}, bf16[3584,2048]{1,0:T(8,128)(2,1)}, u32[]{:S(2)}) copy-start(bf16[3584,2048]{1,0:T(8,128)(2,1)} %multiply_convert_fusion) | copy-start | bytes 44040196
  183.6 1.5 collective-permute-start
  185.1 14.8 %collective-permute-start.1 = (f32[3584,16]{0,1:T(8,128)S(1)}, f32[3584,16]{0,1:T(8,128)S(1)}, u32[]{:S(2)}, u32[]{:S(2)}) collective-permute-start(f32[3584,16]{0,1:T(8,128)S(1)} %add.46), channel_id=1, source_target_pairs={{0,2},{1,3},{2,0},{3,1},{4,6},{5,7},{6,4},{7,5},{8,10},{9,11},{10,... | collective-permute-start | bytes 688136 | tf_op jit(solution)/shard_map/ppermute | solution.py:82
Sparse Core Ops, SparseCore 0:
  10.1 51.7 all-gather.4
  63.5 29.9 all-gather.2
  147.1 73.5 reduce-scatter.1
  224.5 70.3 all-reduce.1
